TPU v7x, 32 devices: a whole 2x2x4 slice. The times are simulated.
32 devices in a mesh: sample: 4 (over z), tensor: 2 (over y), section: 4 (over x, core).
Axes of the slice: x: 2, y: 2, z: 4, core: 2. Of those that a mesh axis runs over, the one named last changes fastest.
Arguments:
- hidden_in: bfloat16 [512, 8192], P('sample', 'section'), may hold values from -6 to 6
- token_ids: int32 [512], P('sample'), may hold values from 0 to 128255, as said below
- mlp_gain: bfloat16 [8192], P('section'), may hold values from 0.099609375 to 1.8984375
- attn_gain: bfloat16 [8192], P('section'), may hold values from 0.099609375 to 1.8984375
- gate_weight: bfloat16 [28672, 8192], P(('sample', 'tensor'), 'section'), may hold values from -0.0625 to 0.0625
- up_weight: bfloat16 [28672, 8192], P(('sample', 'tensor'), 'section'), may hold values from -0.0625 to 0.0625
- down_weight: bfloat16 [28672, 8192], P(('sample', 'tensor'), 'section'), may hold values from -0.03125 to 0.03125
Outputs:
- hidden_out: bfloat16 [512, 8192], P('sample', 'section')
- mlp_cov: float32 [8192, 8192], P('section', ('sample', 'tensor'))
- attn_cov: float32 [8192, 8192], P('section', ('sample', 'tensor'))
Inputs may be any that keep to these rules, and one draw needn't show every extreme that they name: `token_ids`: 0 is padding and is left out of the statistics; within each block of 128 rows the padding forms the tail, and the last block has none.
All inputs are finite; a program needn't handle non-finite values.
Results may differ from a plain program's by a relative error of at most 0.0071.
Values may be sent and summed in bfloat16 or wider, within the bound.
A program may use at most 256 MiB of HBM per device.

v0:
```python
import jax
import jax.numpy as jnp
from jax import lax
from jax.sharding import PartitionSpec as P

D = 8192
EPS = 1e-05
ROW_CONTRACT = (((1,), (1,)), ((), ()))
TOKEN_CONTRACT = (((0,), (0,)), ((), ()))


def broadcast(block, axis, source):
    block = jnp.where(lax.axis_index(axis) == source, block, jnp.zeros_like(block))
    return lax.psum(block, axis)


def rms_norm(values, totals, gain):
    scales = lax.rsqrt(totals / D + EPS)
    return (values * scales[:, None] * gain.astype(jnp.float32)).astype(jnp.bfloat16)


def covariance(rows_in, columns, live_mask, live_count):
    weighted = rows_in * live_mask[:, None]
    products = lax.dot_general(
        weighted, columns, TOKEN_CONTRACT, preferred_element_type=jnp.float32
    )
    row_means = jnp.dot(live_mask, rows_in, preferred_element_type=jnp.float32) / live_count
    col_means = jnp.dot(live_mask, columns, preferred_element_type=jnp.float32) / live_count
    return products / live_count - row_means[:, None] * col_means[None, :]


def local(hidden_in, token_ids, mlp_gain, attn_gain, gate_weight, up_weight, down_weight):
    n_sample = lax.axis_size("sample")
    n_tensor = lax.axis_size("tensor")
    panel = hidden_in.shape[1]
    tok_local = hidden_in.shape[0]
    col_width = D // (n_sample * n_tensor)
    column_index = lax.axis_index("sample") * n_tensor + lax.axis_index("tensor")
    owner_section = column_index * col_width // panel
    column_start = column_index * col_width - owner_section * panel
    values = hidden_in.astype(jnp.float32)
    totals = lax.psum(jnp.sum(values * values, axis=1), "section")
    mlp_input = rms_norm(values, totals, mlp_gain)
    live_local = (token_ids != 0).astype(jnp.bfloat16)
    rows_in, mask_rows = lax.all_gather((mlp_input, live_local), "sample", axis=0, tiled=True)
    gate_part = lax.dot_general(
        rows_in, gate_weight, ROW_CONTRACT, preferred_element_type=jnp.float32
    )
    up_part = lax.dot_general(rows_in, up_weight, ROW_CONTRACT, preferred_element_type=jnp.float32)
    mlp_rows, live_mask, gate_part, up_part = (rows_in, mask_rows, gate_part, up_part)
    live_count = jnp.sum(live_mask.astype(jnp.float32))
    gate_share, up_share = (
        lax.psum_scatter(gate_part, "section", scatter_dimension=0, tiled=True),
        lax.psum_scatter(up_part, "section", scatter_dimension=0, tiled=True),
    )
    share_units = (jax.nn.silu(gate_share) * up_share).astype(jnp.bfloat16)
    hidden_units = lax.all_gather(share_units, "section", axis=0, tiled=True)
    share_rows = tok_local // n_tensor
    residual = lax.psum_scatter(
        jnp.dot(hidden_units, down_weight, preferred_element_type=jnp.float32),
        ("sample", "tensor"),
        scatter_dimension=0,
        tiled=True,
    )
    own_rows = lax.dynamic_slice_in_dim(
        values, lax.axis_index("tensor") * share_rows, share_rows, 0
    )
    updated = (own_rows + residual).astype(jnp.bfloat16)
    hidden_out = lax.all_gather(updated, "tensor", axis=0, tiled=True)
    out_values = hidden_out.astype(jnp.float32)
    out_totals = lax.psum(jnp.sum(out_values * out_values, axis=1), "section")
    attn_input = rms_norm(out_values, out_totals, attn_gain)
    mlp_pick = lax.dynamic_slice_in_dim(mlp_rows, column_start, col_width, 1)
    mlp_columns = broadcast(mlp_pick, "section", owner_section)
    mlp_cov = covariance(mlp_rows, mlp_columns, live_mask, live_count)
    attn_rows = lax.all_gather(attn_input, "sample", axis=0, tiled=True)
    attn_pick = lax.dynamic_slice_in_dim(attn_rows, column_start, col_width, 1)
    attn_columns = broadcast(attn_pick, "section", owner_section)
    attn_cov = covariance(attn_rows, attn_columns, live_mask, live_count)
    return (hidden_out, mlp_cov, attn_cov)


def solution(mesh):
    in_specs = (
        P("sample", "section"),
        P("sample"),
        P("section"),
        P("section"),
        P(("sample", "tensor"), "section"),
        P(("sample", "tensor"), "section"),
        P(("sample", "tensor"), "section"),
    )
    out_specs = (
        P("sample", "section"),
        P("section", ("sample", "tensor")),
        P("section", ("sample", "tensor")),
    )
    return jax.shard_map(local, mesh=mesh, in_specs=in_specs, out_specs=out_specs, check_vma=False)
```

profile of v0, /device:TPU:0, one launch (start us, length us, event | category | flops | bytes accessed | tf_op | source)
XLA Modules:
  0.0 492.0 jit_solution(1465766490819151199)
XLA Ops:
  7.2 0.0 all-gather.5.cloned.1.call-start
  7.2 1.2 multiply_reduce_fusion
  8.4 8.4 %psum.28 = f32[128]{0:T(128)S(1)} all-reduce(f32[128]{0:T(128)S(1)} %multiply_reduce_fusion), channel_id=1, replica_groups=mesh['sample'=4,'tensor'=2,'section'=4] {'section'}, use_global_device_ids=true, to_apply=%region_1.2 | all-reduce | flops 128 | bytes 1024 | tf_op jit(solution)/shard_map/psum | solution.py:42
  16.8 0.7 convert_element_type.31
  17.5 2.0 multiply_convert_fusion.1
  19.5 0.0 all-gather.5.cloned.1.call-update
  19.6 0.0 reduce-scatter.6.cloned.1.call-start
  19.6 46.1 %all-gather.5.cloned.1.call-done = bf16[512,2048]{1,0:T(8,128)(2,1)} async-done(((bf16[128,2048]{1,0:T(8,128)(2,1)}), bf16[512,2048]{1,0:T(8,128)(2,1)}) %all-gather.5.cloned.1.call-update) | async-done | bytes 2097168 | tf_op jit(solution)/shard_map/all_gather | solution.py:45
  65.7 13.5 %fusion.17 = f32[512,3584]{1,0:T(8,128)} fusion(bf16[512,2048]{1,0:T(8,128)(2,1)} %all-gather.5.cloned.1.call-done, bf16[3584,2048]{1,0:T(8,128)(2,1)} %param.12), kind=kOutput, calls=%fused_computation.35 | convolution fusion | flops 7516192768 | bytes 24117248 | tf_op jit(solution)/shard_map/dot_general | solution.py:49
  79.2 0.0 copy-start.1
  79.2 0.0 reduce-scatter.6.cloned.1.call-update
  79.2 0.0 reduce-scatter.4.cloned.1.call-start
  79.3 1.5 copy-done.1
  80.8 13.3 %fusion.16 = f32[512,3584]{1,0:T(8,128)} fusion(bf16[512,2048]{1,0:T(8,128)(2,1)S(1)} %copy-done.1, bf16[3584,2048]{1,0:T(8,128)(2,1)} %param.11), kind=kOutput, calls=%fused_computation.34 | convolution fusion | flops 7516192768 | bytes 24117248 | tf_op jit(solution)/shard_map/dot_general | solution.py:46
  94.1 0.0 reduce-scatter.4.cloned.1.call-update
  94.1 0.0 all-gather.7.cloned.1.call-start
  94.2 50.0 %reduce-scatter.6.cloned.1.call-done = f32[128,3584]{1,0:T(8,128)} async-done(((f32[512,3584]{1,0:T(8,128)}), f32[128,3584]{1,0:T(8,128)}) %reduce-scatter.6.cloned.1.call-update) | async-done | bytes 1835024 | tf_op jit(solution)/shard_map/reduce_scatter | solution.py:54
  144.2 69.1 %reduce-scatter.4.cloned.1.call-done = f32[128,3584]{1,0:T(8,128)} async-done(((f32[512,3584]{1,0:T(8,128)}), f32[128,3584]{1,0:T(8,128)}) %reduce-scatter.4.cloned.1.call-update) | async-done | bytes 1835024 | tf_op jit(solution)/shard_map/reduce_scatter | solution.py:53
  213.3 3.5 multiply_convert_fusion
  216.7 0.0 all-gather.7.cloned.1.call-update
  216.8 0.0 reduce-scatter.8.cloned.1.call-start
  216.8 31.6 %all-gather.7.cloned.1.call-done = bf16[512,3584]{1,0:T(8,128)(2,1)} async-done(((bf16[128,3584]{1,0:T(8,128)(2,1)}), bf16[512,3584]{1,0:T(8,128)(2,1)}) %all-gather.7.cloned.1.call-update) | async-done | bytes 3670032 | tf_op jit(solution)/shard_map/all_gather | solution.py:57
  248.4 13.4 %fusion.18 = f32[512,2048]{1,0:T(8,128)} fusion(bf16[512,3584]{1,0:T(8,128)(2,1)} %all-gather.7.cloned.1.call-done, bf16[3584,2048]{1,0:T(8,128)(2,1)} %param.13), kind=kOutput, calls=%fused_computation.36 | convolution fusion | flops 7516192768 | bytes 22544384 | tf_op jit(solution)/shard_map/dot_general | solution.py:60
  261.7 0.0 copy-start
  261.7 0.0 copy-start.3
  261.7 0.0 reduce-scatter.8.cloned.1.call-update
  261.8 0.0 copy-start.4
  261.8 0.0 all-gather.9.cloned.1.call-start
  261.8 0.9 copy-done
  262.8 1.1 convert_element_type.30
  263.9 0.0 copy-done.3
  263.9 86.8 %reduce-scatter.8.cloned.1.call-done = f32[64,2048]{1,0:T(8,128)} async-done(((f32[512,2048]{1,0:T(8,128)}), f32[64,2048]{1,0:T(8,128)}) %reduce-scatter.8.cloned.1.call-update) | async-done | bytes 524304 | tf_op jit(solution)/shard_map/reduce_scatter | solution.py:59
  350.6 1.3 add_convert_fusion
  351.9 8.3 %all_gather.17 = bf16[128,2048]{1,0:T(8,128)(2,1)S(1)} all-gather(bf16[64,2048]{1,0:T(8,128)(2,1)S(1)} %add_convert_fusion), channel_id=1, replica_groups=mesh['sample'=4,'tensor'=2,'section'=4] {'tensor'}, dimensions={0}, use_global_device_ids=true | all-gather | bytes 786432 | tf_op jit(solution)/shard_map/all_gather | solution.py:69
  360.2 0.2 fusion.2
  360.4 5.7 %psum.30 = f32[128]{0:T(128)S(1)} all-reduce(f32[128]{0:T(128)S(1)} %fusion.2), channel_id=1, replica_groups=mesh['sample'=4,'tensor'=2,'section'=4] {'section'}, use_global_device_ids=true, to_apply=%region_8.9 | all-reduce | flops 128 | bytes 1024 | tf_op jit(solution)/shard_map/psum | solution.py:71
  366.1 1.0 fusion.4
  367.0 0.0 all-gather.9.cloned.1.call-update
  367.1 0.0 all-reduce.3.cloned.1.call-start
  367.1 0.0 copy-done.4
  367.2 10.6 %all-gather = bf16[4,1,128]{2,1,0:T(2,128)(2,1)S(1)} all-gather(bf16[1,1,128]{2,1,0:T(2,128)(2,1)S(1)} %fusion.15), channel_id=1, replica_groups=mesh['sample'=4,'tensor'=2,'section'=4] {'sample'}, dimensions={0}, use_global_device_ids=true | all-gather | bytes 1280 | tf_op jit(solution)/shard_map/all_gather | solution.py:45
  377.8 1.2 dynamic-slice_select_fusion.1
  379.0 34.4 %all-gather.9.cloned.1.call-done = bf16[512,2048]{1,0:T(8,128)(2,1)} async-done(((bf16[128,2048]{1,0:T(8,128)(2,1)}), bf16[512,2048]{1,0:T(8,128)(2,1)}) %all-gather.9.cloned.1.call-update) | async-done | bytes 2097168 | tf_op jit(solution)/shard_map/all_gather | solution.py:76
  413.4 2.4 dynamic-slice_select_fusion
  415.8 0.0 all-reduce.3.cloned.1.call-update
  415.8 0.6 convert_reduce_fusion
  416.4 0.4 fusion.13
  416.8 0.7 broadcast_divide_fusion.1
  417.5 2.0 fusion.9
  419.4 0.7 broadcast_divide_fusion
  420.1 46.5 %all-reduce.3.cloned.1.call-done = (bf16[512,1024]{1,0:T(8,128)(2,1)}, bf16[512,1024]{1,0:T(8,128)(2,1)}) async-done(((bf16[512,1024]{1,0:T(8,128)(2,1)}, bf16[512,1024]{1,0:T(8,128)(2,1)}), (bf16[512,1024]{1,0:T(8,128)(2,1)}, bf16[512,1024]{1,0:T(8,128)(2,1)})) %all-reduce.3.cloned.1.call-update) | async-done | bytes 2097168 | tf_op jit(solution)/shard_map/psum | solution.py:14
  466.6 1.5 fusion.11
  468.1 1.5 fusion.7
  469.6 0.7 broadcast_divide_fusion.2
  470.3 0.0 copy-start.2
  470.3 8.6 %multiply_subtract_fusion = f32[2048,1024]{1,0:T(8,128)} fusion(f32[1024]{0:T(1024)S(1)} %get-tuple-element.5, f32[2048]{0:T(1024)S(1)} %broadcast_divide_fusion, f32[]{:T(128)} %convert_reduce_fusion, bf16[512,1024]{1,0:T(8,128)(2,1)} %get-tuple-element.4, bf16[512,2048]{1,0:T(8,128)(2,1)} %all-gather.9.cloned.1.call-done, bf16[512]{0:T(512)(128)(2,1)S(1)} %bitcast.33), kind=kOutput, calls=%fused_computation | convolution fusion | flops 2154823680 | bytes 11547652 | tf_op jit(solution)/shard_map/dot_general | solution.py:24
  478.9 0.0 copy-done.2
  478.9 5.5 %multiply_subtract_fusion.1 = f32[2048,1024]{1,0:T(8,128)} fusion(f32[1024]{0:T(1024)S(1)} %get-tuple-element.6, f32[2048]{0:T(1024)S(1)} %broadcast_divide_fusion.1, f32[]{:T(128)} %convert_reduce_fusion, bf16[512,1024]{1,0:T(8,128)(2,1)S(1)} %copy-done.2, bf16[512,2048]{1,0:T(8,128)(2,1)S(1)} %copy-done.1, bf16[512]{0:T(512)(128)(2,1)S(1)} %bitcast.34), kind=kOutput, calls=%fused_computation.1 | convolution fusion | flops 2154823680 | bytes 11547652 | tf_op jit(solution)/shard_map/dot_general | solution.py:24
  484.4 0.8 copy.13
  (5 shorter events, 0.0 us)
Async XLA Ops:
  7.2 58.5 %all-gather.5.cloned.1.call-start = ((), (), s32[]{:S(2)}) async-start(), calls=%async_computation.3 | async-start | bytes 2621440 | tf_op jit(solution)/shard_map/all_gather | solution.py:45
  19.6 124.6 %reduce-scatter.6.cloned.1.call-start = ((), (), s32[]{:S(2)}) async-start(), calls=%async_computation.5 | async-start | bytes 9175040 | tf_op jit(solution)/shard_map/reduce_scatter | solution.py:54
  79.2 1.6 copy-start.1
  79.2 134.0 %reduce-scatter.4.cloned.1.call-start = ((), (), s32[]{:S(2)}) async-start(), calls=%async_computation.4 | async-start | bytes 9175040 | tf_op jit(solution)/shard_map/reduce_scatter | solution.py:53
  94.1 154.3 %all-gather.7.cloned.1.call-start = ((), (), s32[]{:S(2)}) async-start(), calls=%async_computation.6 | async-start | bytes 4587520 | tf_op jit(solution)/shard_map/all_gather | solution.py:57
  216.8 133.9 %reduce-scatter.8.cloned.1.call-start = ((), (), s32[]{:S(2)}) async-start(), calls=%async_computation.7 | async-start | bytes 4718592 | tf_op jit(solution)/shard_map/reduce_scatter | solution.py:59
  261.7 1.0 copy-start
  261.7 2.1 copy-start.3
  261.8 105.4 %copy-start.4 = (s32[128]{0:T(128)S(1)}, s32[128]{0:T(128)}, u32[]{:S(2)}) copy-start(s32[128]{0:T(128)} %param.8) | copy-start | bytes 1540
  261.8 151.6 %all-gather.9.cloned.1.call-start = ((), (), s32[]{:S(2)}) async-start(), calls=%async_computation.8 | async-start | bytes 2621440 | tf_op jit(solution)/shard_map/all_gather | solution.py:76
  367.1 99.6 %all-reduce.3.cloned.1.call-start = ((), (), s32[]{:S(2)}) async-start(), calls=%async_computation.9 | async-start | bytes 4194304 | tf_op jit(solution)/shard_map/psum | solution.py:14
  470.3 8.6 %copy-start.2 = (bf16[512,1024]{1,0:T(8,128)(2,1)S(1)}, bf16[512,1024]{1,0:T(8,128)(2,1)}, u32[]{:S(2)}) copy-start(bf16[512,1024]{1,0:T(8,128)(2,1)} %get-tuple-element.3) | copy-start | bytes 3145732
Sparse Core Ops, SparseCore 0:
  19.7 45.9 all-gather.4
  79.4 64.7 reduce-scatter.5
  147.3 65.9 reduce-scatter.3
  216.9 31.4 all-gather.6
  261.9 88.6 reduce-scatter.7
  367.2 46.1 all-gather.8
  416.4 50.1 all-reduce.2
where the time goes:
time: 493 us; the launch traced here: 492 us
  waiting for transfers between devices  365 us (74%)
  matrix products  59.6 us (12%)
  blocking collectives  33 us (7%)
  other arithmetic  17.1 us (3%)
  between operations  14.2 us (3%)
    reduce_scatter x1, waiting for transfers between devices, local(): lax.psum_scatter(jnp.dot(hidden_units, down_weight, preferred_element_typ...  86.8 us
    reduce_scatter x1, waiting for transfers between devices, local(): lax.psum_scatter(gate_part, 'section', scatter_dimension=0, tiled=True)  69.1 us
    reduce_scatter x1, waiting for transfers between devices, local(): lax.psum_scatter(up_part, 'section', scatter_dimension=0, tiled=True)  50 us
    psum x1, waiting for transfers between devices, broadcast(): return lax.psum(block, axis)  46.5 us
    all_gather x1, waiting for transfers between devices, local(): lax.all_gather((mlp_input, live_local), 'sample', axis=0, tiled=True)  46.1 us
    all_gather x1, waiting for transfers between devices, local(): attn_rows = lax.all_gather(attn_input, 'sample', axis=0, tiled=True)  34.4 us
    all_gather x1, waiting for transfers between devices, local(): hidden_units = lax.all_gather(share_units, 'section', axis=0, tiled=True)  31.6 us
    dot_general x2, matrix products, covariance(): lax.dot_general(weighted, columns, TOKEN_CONTRACT, preferred_element_type...  14.1 us
  transfers between devices with their start and end apart: 7, of which 7 were waited for; matrix products, arithmetic and copies ran while one was open for 4% of the time, Pallas kernels for 0%

commit v1 on v0

--- a/solution.py
+++ b/solution.py
@@ -9,9 +9,15 @@
 TOKEN_CONTRACT = (((0,), (0,)), ((), ()))
 
 
+def summed_here(value, axis):
+    parts = lax.all_gather(value, axis, axis=0, tiled=False)
+    summed = parts.sum(axis=0)
+    return summed
+
+
 def broadcast(block, axis, source):
     block = jnp.where(lax.axis_index(axis) == source, block, jnp.zeros_like(block))
-    return lax.psum(block, axis)
+    return summed_here(block, axis)
 
 
 def rms_norm(values, totals, gain):

time: 493 us -> 506 us (1.026)
  other arithmetic: 17.1 us -> 26.7 us
  waiting for transfers between devices: 365 us -> 372 us
    psum x1 -> x0, waiting for transfers between devices: 46.5 us -> none  [broadcast(): return lax.psum(block, axis)]
    all_gather x0 -> x2, waiting for transfers between devices: none -> 43.5 us  [summed_here(): parts = lax.all_gather(value, axis, axis=0, tiled=False)]
    reduce_scatter x1, waiting for transfers between devices: 50 us -> 69.1 us  [local(): lax.psum_scatter(up_part, 'section', scatter_dimension=0, tiled=True)]
    reduce_scatter x1, waiting for transfers between devices: 69.1 us -> 50 us  [local(): lax.psum_scatter(gate_part, 'section', scatter_dimension=0, tiled=True)]
    all_gather x1, waiting for transfers between devices: 34.4 us -> 45 us  [local(): attn_rows = lax.all_gather(attn_input, 'sample', axis=0, tiled=True)]
    reduce_sum x0 -> x2, other arithmetic: none -> 8.78 us  [summed_here(): summed = parts.sum(axis=0)]
  transfers between devices with their start and end apart: 7 -> 8, of which waited for: 7 -> 8; matrix products, arithmetic and copies ran while one was open for 4% -> 7% of each run, Pallas kernels for 0% -> 0%
where the time goes in v1:
time: 506 us
  waiting for transfers between devices  372 us (74%)
  matrix products  57.6 us (11%)
  blocking collectives  31.5 us (6%)
  other arithmetic  26.7 us (5%)
  between operations  14.2 us (3%)
    reduce_scatter x1, waiting for transfers between devices, local(): lax.psum_scatter(jnp.dot(hidden_units, down_weight, preferred_element_typ...  86.8 us
    reduce_scatter x1, waiting for transfers between devices, local(): lax.psum_scatter(up_part, 'section', scatter_dimension=0, tiled=True)  69.1 us
    reduce_scatter x1, waiting for transfers between devices, local(): lax.psum_scatter(gate_part, 'section', scatter_dimension=0, tiled=True)  50 us
    all_gather x1, waiting for transfers between devices, local(): lax.all_gather((mlp_input, live_local), 'sample', axis=0, tiled=True)  46.1 us
    all_gather x1, waiting for transfers between devices, local(): attn_rows = lax.all_gather(attn_input, 'sample', axis=0, tiled=True)  45 us
    all_gather x2, waiting for transfers between devices, summed_here(): parts = lax.all_gather(value, axis, axis=0, tiled=False)  43.5 us
    all_gather x1, waiting for transfers between devices, local(): hidden_units = lax.all_gather(share_units, 'section', axis=0, tiled=True)  31.6 us
    dot_general x2, matrix products, covariance(): lax.dot_general(weighted, columns, TOKEN_CONTRACT, preferred_element_type...  13.7 us
  transfers between devices with their start and end apart: 8, of which 8 were waited for; matrix products, arithmetic and copies ran while one was open for 7% of the time, Pallas kernels for 0%

profile of v1, /device:TPU:0, one launch (start us, length us, event | category | flops | bytes accessed | tf_op | source)
XLA Modules:
  0.0 505.8 jit_solution(8545747548678195092)
XLA Ops:
  7.2 0.0 all-gather.9.cloned.1.call-start
  7.2 0.7 convert_element_type.35
  7.9 1.2 multiply_reduce_fusion
  9.1 8.4 %psum.14 = f32[128]{0:T(128)S(1)} all-reduce(f32[128]{0:T(128)S(1)} %multiply_reduce_fusion), channel_id=1, replica_groups=mesh['sample'=4,'tensor'=2,'section'=4] {'section'}, use_global_device_ids=true, to_apply=%region_1.2 | all-reduce | flops 128 | bytes 1024 | tf_op jit(solution)/shard_map/psum | solution.py:48
  17.5 2.0 multiply_convert_fusion.1
  19.5 0.0 all-gather.9.cloned.1.call-update
  19.6 0.0 reduce-scatter.4.cloned.1.call-start
  19.6 46.1 %all-gather.9.cloned.1.call-done = bf16[512,2048]{1,0:T(8,128)(2,1)} async-done(((bf16[128,2048]{1,0:T(8,128)(2,1)}), bf16[512,2048]{1,0:T(8,128)(2,1)}) %all-gather.9.cloned.1.call-update) | async-done | bytes 2097168 | tf_op jit(solution)/shard_map/all_gather | solution.py:51
  65.7 13.5 %fusion.16 = f32[512,3584]{1,0:T(8,128)} fusion(bf16[512,2048]{1,0:T(8,128)(2,1)} %all-gather.9.cloned.1.call-done, bf16[3584,2048]{1,0:T(8,128)(2,1)} %param.11), kind=kOutput, calls=%fused_computation.34 | convolution fusion | flops 7516192768 | bytes 24117248 | tf_op jit(solution)/shard_map/dot_general | solution.py:52
  79.2 0.0 copy-start.1
  79.2 0.0 reduce-scatter.4.cloned.1.call-update
  79.2 0.0 reduce-scatter.6.cloned.1.call-start
  79.3 1.5 copy-done.1
  80.8 13.3 %fusion.17 = f32[512,3584]{1,0:T(8,128)} fusion(bf16[512,2048]{1,0:T(8,128)(2,1)S(1)} %copy-done.1, bf16[3584,2048]{1,0:T(8,128)(2,1)} %param.12), kind=kOutput, calls=%fused_computation.35 | convolution fusion | flops 7516192768 | bytes 24117248 | tf_op jit(solution)/shard_map/dot_general | solution.py:55
  94.1 0.0 reduce-scatter.6.cloned.1.call-update
  94.1 0.0 all-gather.11.cloned.1.call-start
  94.2 50.0 %reduce-scatter.4.cloned.1.call-done = f32[128,3584]{1,0:T(8,128)} async-done(((f32[512,3584]{1,0:T(8,128)}), f32[128,3584]{1,0:T(8,128)}) %reduce-scatter.4.cloned.1.call-update) | async-done | bytes 1835024 | tf_op jit(solution)/shard_map/reduce_scatter | solution.py:59
  144.2 69.1 %reduce-scatter.6.cloned.1.call-done = f32[128,3584]{1,0:T(8,128)} async-done(((f32[512,3584]{1,0:T(8,128)}), f32[128,3584]{1,0:T(8,128)}) %reduce-scatter.6.cloned.1.call-update) | async-done | bytes 1835024 | tf_op jit(solution)/shard_map/reduce_scatter | solution.py:60
  213.3 3.5 multiply_convert_fusion
  216.7 0.0 all-gather.11.cloned.1.call-update
  216.8 0.0 reduce-scatter.8.cloned.1.call-start
  216.8 31.6 %all-gather.11.cloned.1.call-done = bf16[512,3584]{1,0:T(8,128)(2,1)} async-done(((bf16[128,3584]{1,0:T(8,128)(2,1)}), bf16[512,3584]{1,0:T(8,128)(2,1)}) %all-gather.11.cloned.1.call-update) | async-done | bytes 3670032 | tf_op jit(solution)/shard_map/all_gather | solution.py:63
  248.4 13.4 %fusion.18 = f32[512,2048]{1,0:T(8,128)} fusion(bf16[512,3584]{1,0:T(8,128)(2,1)} %all-gather.11.cloned.1.call-done, bf16[3584,2048]{1,0:T(8,128)(2,1)} %param.13), kind=kOutput, calls=%fused_computation.36 | convolution fusion | flops 7516192768 | bytes 22544384 | tf_op jit(solution)/shard_map/dot_general | solution.py:66
  261.7 0.0 copy-start
  261.7 0.0 reduce-scatter.8.cloned.1.call-update
  261.8 0.0 all-gather.13.cloned.1.call-start
  261.8 1.0 copy-done
  262.8 1.1 convert_element_type.34
  263.9 0.0 copy-done.4
  263.9 86.8 %reduce-scatter.8.cloned.1.call-done = f32[64,2048]{1,0:T(8,128)} async-done(((f32[512,2048]{1,0:T(8,128)}), f32[64,2048]{1,0:T(8,128)}) %reduce-scatter.8.cloned.1.call-update) | async-done | bytes 524304 | tf_op jit(solution)/shard_map/reduce_scatter | solution.py:65
  350.6 1.3 add_convert_fusion
  351.9 8.3 %all_gather.29 = bf16[128,2048]{1,0:T(8,128)(2,1)S(1)} all-gather(bf16[64,2048]{1,0:T(8,128)(2,1)S(1)} %add_convert_fusion), channel_id=1, replica_groups=mesh['sample'=4,'tensor'=2,'section'=4] {'tensor'}, dimensions={0}, use_global_device_ids=true | all-gather | bytes 786432 | tf_op jit(solution)/shard_map/all_gather | solution.py:75
  360.2 0.2 fusion.2
  360.4 5.7 %psum.15 = f32[128]{0:T(128)S(1)} all-reduce(f32[128]{0:T(128)S(1)} %fusion.2), channel_id=1, replica_groups=mesh['sample'=4,'tensor'=2,'section'=4] {'section'}, use_global_device_ids=true, to_apply=%region_8.9 | all-reduce | flops 128 | bytes 1024 | tf_op jit(solution)/shard_map/psum | solution.py:77
  366.1 1.0 fusion.4
  367.0 0.0 all-gather.13.cloned.1.call-update
  367.1 0.0 all-gather.15.cloned.1.call-start
  367.1 1.2 dynamic-slice_select_fusion.1
  368.4 0.0 all-gather.15.cloned.1.call-update
  368.4 0.0 all-gather.17.cloned.1.call-start
  368.4 45.0 %all-gather.13.cloned.1.call-done = bf16[512,2048]{1,0:T(8,128)(2,1)} async-done(((bf16[128,2048]{1,0:T(8,128)(2,1)}), bf16[512,2048]{1,0:T(8,128)(2,1)}) %all-gather.13.cloned.1.call-update) | async-done | bytes 2097168 | tf_op jit(solution)/shard_map/all_gather | solution.py:82
  413.4 2.4 dynamic-slice_select_fusion
  415.8 0.0 all-gather.17.cloned.1.call-update
  415.8 0.0 copy-done.5
  415.9 9.1 %all-gather.2 = bf16[4,1,128]{2,1,0:T(2,128)(2,1)S(1)} all-gather(bf16[1,1,128]{2,1,0:T(2,128)(2,1)S(1)} %fusion.15), channel_id=1, replica_groups=mesh['sample'=4,'tensor'=2,'section'=4] {'sample'}, dimensions={0}, use_global_device_ids=true | all-gather | bytes 1280 | tf_op jit(solution)/shard_map/all_gather | solution.py:51
  425.0 0.6 convert_reduce_fusion
  425.6 0.4 fusion.13
  426.0 0.7 broadcast_divide_fusion.1
  426.7 22.2 %all-gather.15.cloned.1.call-done = bf16[2048,1024]{1,0:T(8,128)(2,1)} async-done(((bf16[512,1024]{1,0:T(8,128)(2,1)}), bf16[2048,1024]{1,0:T(8,128)(2,1)}) %all-gather.15.cloned.1.call-update) | async-done | bytes 4194320 | tf_op jit(solution)/shard_map/all_gather | solution.py:13
  448.8 4.4 reduce_sum.52
  453.2 1.5 fusion.11
  454.7 0.7 broadcast_divide_fusion.3
  455.3 0.0 copy-start.2
  455.4 7.0 %multiply_subtract_fusion.1 = f32[2048,1024]{1,0:T(8,128)} fusion(f32[1024]{0:T(1024)S(1)} %broadcast_divide_fusion.3, f32[2048]{0:T(1024)S(1)} %broadcast_divide_fusion.1, f32[]{:T(128)} %convert_reduce_fusion, bf16[512,1024]{1,0:T(8,128)(2,1)} %reduce_sum.52, bf16[512,2048]{1,0:T(8,128)(2,1)S(1)} %copy-done.1, bf16[512]{0:T(512)(128)(2,1)S(1)} %bitcast.37), kind=kOutput, calls=%fused_computation.1 | convolution fusion | flops 2154823680 | bytes 11547652 | tf_op jit(solution)/shard_map/dot_general | solution.py:30
  462.4 0.0 copy-done.2
  462.4 0.4 fusion.9
  462.7 0.8 broadcast_divide_fusion
  463.6 21.3 %all-gather.17.cloned.1.call-done = bf16[2048,1024]{1,0:T(8,128)(2,1)} async-done(((bf16[512,1024]{1,0:T(8,128)(2,1)}), bf16[2048,1024]{1,0:T(8,128)(2,1)}) %all-gather.17.cloned.1.call-update) | async-done | bytes 4194320 | tf_op jit(solution)/shard_map/all_gather | solution.py:13
  484.9 4.4 reduce_sum.55
  489.3 1.5 fusion.7
  490.7 0.7 broadcast_divide_fusion.2
  491.4 0.0 copy-done.3
  491.4 6.7 %multiply_subtract_fusion = f32[2048,1024]{1,0:T(8,128)} fusion(f32[1024]{0:T(1024)S(1)} %broadcast_divide_fusion.2, f32[2048]{0:T(1024)S(1)} %broadcast_divide_fusion, f32[]{:T(128)} %convert_reduce_fusion, bf16[512,1024]{1,0:T(8,128)(2,1)} %reduce_sum.55, bf16[512,2048]{1,0:T(8,128)(2,1)S(1)} %copy-done.3, bf16[512]{0:T(512)(128)(2,1)S(1)} %bitcast.38), kind=kOutput, calls=%fused_computation | convolution fusion | flops 2154823680 | bytes 11547652 | tf_op jit(solution)/shard_map/dot_general | solution.py:30
  498.1 0.8 copy.11
  (8 shorter events, 0.0 us)
Async XLA Ops:
  7.2 58.5 %all-gather.9.cloned.1.call-start = ((), (), s32[]{:S(2)}) async-start(), calls=%async_computation.3 | async-start | bytes 2621440 | tf_op jit(solution)/shard_map/all_gather | solution.py:51
  19.6 124.6 %reduce-scatter.4.cloned.1.call-start = ((), (), s32[]{:S(2)}) async-start(), calls=%async_computation.4 | async-start | bytes 9175040 | tf_op jit(solution)/shard_map/reduce_scatter | solution.py:59
  79.2 1.6 copy-start.1
  79.2 134.0 %reduce-scatter.6.cloned.1.call-start = ((), (), s32[]{:S(2)}) async-start(), calls=%async_computation.5 | async-start | bytes 9175040 | tf_op jit(solution)/shard_map/reduce_scatter | solution.py:60
  94.1 154.3 %all-gather.11.cloned.1.call-start = ((), (), s32[]{:S(2)}) async-start(), calls=%async_computation.6 | async-start | bytes 4587520 | tf_op jit(solution)/shard_map/all_gather | solution.py:63
  216.8 133.9 %reduce-scatter.8.cloned.1.call-start = ((), (), s32[]{:S(2)}) async-start(), calls=%async_computation.7 | async-start | bytes 4718592 | tf_op jit(solution)/shard_map/reduce_scatter | solution.py:65
  261.7 1.0 copy-start
  261.7 2.1 copy-start.4
  261.8 151.6 %all-gather.13.cloned.1.call-start = ((), (), s32[]{:S(2)}) async-start(), calls=%async_computation.8 | async-start | bytes 2621440 | tf_op jit(solution)/shard_map/all_gather | solution.py:82
  367.0 48.8 %copy-start.5 = (s32[128]{0:T(128)S(1)}, s32[128]{0:T(128)}, u32[]{:S(2)}) copy-start(s32[128]{0:T(128)} %param.8) | copy-start | bytes 1540
  367.1 81.8 %all-gather.15.cloned.1.call-start = ((), (), s32[]{:S(2)}) async-start(), calls=%async_computation.9 | async-start | bytes 5242880 | tf_op jit(solution)/shard_map/all_gather | solution.py:13
  368.4 116.5 %all-gather.17.cloned.1.call-start = ((), (), s32[]{:S(2)}) async-start(), calls=%async_computation.10 | async-start | bytes 5242880 | tf_op jit(solution)/shard_map/all_gather | solution.py:13
  455.3 7.0 %copy-start.2 = (bf16[512,2048]{1,0:T(8,128)(2,1)S(1)}, bf16[512,2048]{1,0:T(8,128)(2,1)}, u32[]{:S(2)}) copy-start(bf16[512,2048]{1,0:T(8,128)(2,1)} %all-gather.13.cloned.1.call-done) | copy-start | bytes 6291460
  462.7 28.7 %copy-start.3 = (bf16[512,2048]{1,0:T(8,128)(2,1)S(1)}, bf16[512,2048]{1,0:T(8,128)(2,1)}, u32[]{:S(2)}) copy-start(bf16[512,2048]{1,0:T(8,128)(2,1)} %all-gather.13.cloned.1.call-done) | copy-start | bytes 6291460
Sparse Core Ops, SparseCore 0:
  19.7 45.9 all-gather.8
  79.4 64.7 reduce-scatter.3
  147.3 65.9 reduce-scatter.5
  216.9 31.4 all-gather.10
  261.9 88.6 reduce-scatter.7
  367.2 46.1 all-gather.12
  415.5 33.2 all-gather.14
  450.4 34.4 all-gather.16
